TPU v7x, 32 devices: a whole 2x2x4 slice. The times are simulated.
32 devices in a mesh: ctx: 4 (over z), exp: 8 (over y, x, core).
Axes of the slice: x: 2, y: 2, z: 4, core: 2. Of those that a mesh axis runs over, the one named last changes fastest.
Arguments:
- resid_input: bfloat16 [512, 4096], P(('ctx', 'exp')), may hold values from -80 to 80
- norm_gain: float32 [4096], replicated, may hold values from 0.1 to 1.9
- expert_ids: int32 [512, 2], P(('ctx', 'exp')), may hold values from 0 to 3, all different within a row
- route_probs: bfloat16 [512, 2], P(('ctx', 'exp')), may hold values from 0.19921875 to 0.796875
- gate_weight: bfloat16 [8, 6144, 4096], P('exp', 'ctx'), may hold values from -0.09375 to 0.09375
- up_weight: bfloat16 [8, 6144, 4096], P('exp', 'ctx'), may hold values from -0.09375 to 0.09375
- down_weight: bfloat16 [8, 6144, 4096], P('exp', 'ctx'), may hold values from -0.09375 to 0.09375
- grad_output: bfloat16 [512, 4096], P('ctx', 'exp'), may hold values from -6 to 6
- mixer_input: bfloat16 [512, 4096], P('ctx', 'exp'), may hold values from -0.29882812 to 0.29882812
- state_input: bfloat16 [512, 2048], P('ctx', 'exp'), may hold values from -0.5 to 0.5
- state_output: bfloat16 [512, 2048], P('ctx', 'exp'), may hold values from -0.119628906 to 0.119628906
- step_size: float32 [512, 64], P('ctx', 'exp'), may hold values from 0.3 to 1.5
- log_retention: float32 [512, 64], P('ctx', 'exp'), may hold values from -1.5 to 0, as said below
- skip_gain: float32 [64], P('exp'), may hold values from 0.5 to 1.5
Outputs:
- resid_grad: bfloat16 [512, 4096], P('ctx', 'exp')
- mixer_grad: bfloat16 [512, 4096], P('ctx', 'exp')
- state_input_grad: float32 [512, 2048], P('ctx', 'exp')
Inputs may be any that keep to these rules, and one draw needn't show every extreme that they name: `expert_ids`: each token names 2 different experts. `log_retention`: strictly negative.
All inputs are finite; a program needn't handle non-finite values.
Results may differ from a plain program's by a relative error of at most 0.009.
Values may be sent and summed in bfloat16 or wider, within the bound.
No kernel may reach another device: no remote copies, remote signals or barrier semaphores. Data moves between devices by JAX's collectives and lax.ppermute only.
A program may use at most 128 MiB of HBM per device.

v0:
```python
from functools import partial
import jax
import jax.numpy as jnp
from jax import lax
from jax.sharding import PartitionSpec as P

N = 128
highest = lax.Precision.HIGHEST
norm_epsilon = 1e-05


def carried_in(shard, axis, join, neutral):
    count = lax.axis_size(axis)
    place = lax.axis_index(axis)
    ahead = count - 1 - place
    gathered = jax.tree.map(
        lambda a, kind: lax.all_gather(a.astype(kind), axis), shard, (jnp.bfloat16, jnp.bfloat16)
    )
    state = jax.tree.map(lambda a, e: jnp.zeros_like(a) + jnp.asarray(e, a.dtype), shard, neutral)

    def one(hop, state):
        source = count - 1 - hop
        return join(
            state,
            jax.tree.map(
                lambda a, own: lax.dynamic_index_in_dim(a, source, 0, False).astype(own.dtype),
                gathered,
                shard,
            ),
        )

    return lax.fori_loop(0, ahead, one, state)


def expert_slots(flat_ids, expert, capacity):
    matches = (flat_ids == expert).astype(jnp.int32)
    position = jnp.cumsum(matches) - matches
    slot_numbers = jnp.arange(capacity, dtype=jnp.int32)[:, None]
    picked = (position[None, :] == slot_numbers) & (matches[None, :] > 0)
    return picked.astype(jnp.bfloat16)


def mixer_setup(input_states, output_states, log_retention):
    token_count = log_retention.shape[0]
    cumulative = jnp.cumsum(log_retention, axis=0)
    later_mask = jnp.arange(token_count)[None, :] >= jnp.arange(token_count)[:, None]
    difference = cumulative.T[:, None, :] - cumulative.T[:, :, None]
    decay_matrix = jnp.where(
        later_mask[None], jnp.exp(jnp.where(later_mask[None], difference, 0.0)), 0.0
    )
    intersection = jnp.einsum(
        "tgn,sgn->gts", input_states, output_states, preferred_element_type=jnp.float32
    )
    return (cumulative, decay_matrix, intersection)


def mixer_local(
    upstream, inputs_float, step_size, output_float, cumulative, decay_matrix, intersection
):
    token_count, group_count, state_size = output_float.shape
    head_count = upstream.shape[1]
    head_size = upstream.shape[2]
    head_groups = head_count // group_count
    grouped_up = upstream.reshape(token_count, group_count, head_groups, head_size)
    mixed_weights = (
        decay_matrix.reshape(group_count, head_groups, token_count, token_count)
        * intersection[:, None]
    )
    intra_x = jnp.einsum("gjts,sgjp->tgjp", mixed_weights, grouped_up, precision=highest)
    intra_x = intra_x.reshape(token_count, head_count, head_size)
    inner_product = jnp.einsum("thp,shp->hts", inputs_float, upstream, precision=highest)
    weighted = decay_matrix * inner_product * step_size.T[:, :, None]
    grouped = weighted.reshape(group_count, head_groups, token_count, token_count).sum(axis=1)
    intra_b = jnp.einsum("gts,sgn->tgn", grouped, output_float, precision=highest)
    head_decay = jnp.exp(cumulative).reshape(token_count, group_count, head_groups)
    local_state = jnp.einsum(
        "sgj,sgn,sgjp->gjnp", head_decay, output_float, grouped_up, precision=highest
    )
    return (intra_x, intra_b, local_state.reshape(head_count, state_size, head_size))


def chain_combine(earlier, later):
    return (later[0] * earlier[0], later[1] + later[0][:, None, None] * earlier[1])


def body(
    resid_input,
    norm_gain,
    expert_ids,
    route_probs,
    gate_weight,
    up_weight,
    down_weight,
    grad_output,
    mixer_input,
    state_input,
    state_output,
    step_size,
    log_retention,
    skip_gain,
):
    exp_count = lax.axis_size("exp")
    exp_index = lax.axis_index("exp")
    expert_count = exp_count // 2
    token_rows = resid_input.shape[0]
    row_tokens = token_rows * exp_count
    capacity = 2 * row_tokens // expert_count
    model_width = resid_input.shape[1]
    token_count = mixer_input.shape[0]
    head_count = skip_gain.shape[0]
    head_size = mixer_input.shape[1] // head_count
    group_count = state_input.shape[1] // N
    head_groups = head_count // group_count
    input_states = state_input.reshape(token_count, group_count, N)
    output_states = state_output.reshape(token_count, group_count, N)
    input_float = input_states.astype(jnp.float32)
    output_float = output_states.astype(jnp.float32)
    inputs_float = mixer_input.astype(jnp.float32).reshape(token_count, head_count, head_size)
    cumulative, decay_matrix, intersection = mixer_setup(input_states, output_states, log_retention)
    grad_float = grad_output.astype(jnp.float32)
    all_grad = lax.all_gather(grad_output, "exp", axis=1, tiled=True)
    resid_float = resid_input.astype(jnp.float32)
    inverse_rms = lax.rsqrt(
        jnp.mean(resid_float * resid_float, axis=1, keepdims=True) + norm_epsilon
    )
    scaled_input = resid_float * inverse_rms
    normed_rows = (scaled_input * norm_gain[None, :]).astype(jnp.bfloat16)
    all_normed, all_probs = (
        lax.all_gather(normed_rows, "exp", axis=0, tiled=True),
        lax.all_gather(route_probs, "exp", axis=0, tiled=True),
    )
    all_ids = lax.all_gather(expert_ids, "exp", axis=0, tiled=True)
    flat_ids = all_ids.reshape(-1)
    own_expert = exp_index // 2
    selector = expert_slots(flat_ids, own_expert, capacity)
    token_selector = selector.reshape(capacity, row_tokens, 2).sum(axis=2)
    slot_normed = jnp.dot(token_selector, all_normed, preferred_element_type=jnp.float32).astype(
        jnp.bfloat16
    )
    slot_grad = jnp.dot(token_selector, all_grad, preferred_element_type=jnp.float32).astype(
        jnp.bfloat16
    )
    slot_prob = jnp.dot(selector, all_probs.reshape(-1), preferred_element_type=jnp.float32).astype(
        jnp.bfloat16
    )
    rows_normed, rows_grad, rows_prob = (
        lax.all_gather(slot_normed, "ctx", axis=0, tiled=True),
        lax.all_gather(slot_grad, "ctx", axis=0, tiled=True),
        lax.all_gather(slot_prob, "ctx", axis=0, tiled=True),
    )
    gate_rows = gate_weight[0]
    up_rows = up_weight[0]
    down_rows = down_weight[0]
    contract = (((1,), (1,)), ((), ()))
    gate_pre = lax.dot_general(rows_normed, gate_rows, contract, preferred_element_type=jnp.float32)
    up_pre = lax.dot_general(rows_normed, up_rows, contract, preferred_element_type=jnp.float32)
    hidden_grad = lax.dot_general(
        rows_grad, down_rows, contract, preferred_element_type=jnp.float32
    )
    hidden_grad = hidden_grad * rows_prob.astype(jnp.float32)[:, None]
    sigmoid_gate = jax.nn.sigmoid(gate_pre)
    gate_grad = (
        hidden_grad * up_pre * sigmoid_gate * (1.0 + gate_pre * (1.0 - sigmoid_gate))
    ).astype(jnp.bfloat16)
    up_grad = (hidden_grad * gate_pre * sigmoid_gate).astype(jnp.bfloat16)
    half_sum = lax.psum_scatter(
        (
            jnp.dot(gate_grad, gate_rows, preferred_element_type=jnp.float32)
            + jnp.dot(up_grad, up_rows, preferred_element_type=jnp.float32)
        ).astype(jnp.bfloat16),
        "ctx",
        scatter_dimension=0,
        tiled=True,
    ).astype(jnp.float32)
    all_tables = jax.vmap(partial(expert_slots, flat_ids, capacity=capacity))(
        jnp.arange(expert_count, dtype=jnp.int32)
    )
    token_tables = all_tables.reshape(expert_count, capacity, row_tokens, 2).sum(axis=3)
    own_tables = lax.dynamic_slice_in_dim(token_tables, exp_index * token_rows, token_rows, 2)
    parts = lax.all_gather(half_sum.astype(jnp.bfloat16), "exp", axis=0, tiled=True).astype(
        half_sum.dtype
    )
    owner_tables = jnp.repeat(own_tables, 2, axis=0).astype(jnp.float32)
    route_sum = jnp.einsum(
        "xct,xcd->td",
        owner_tables,
        parts.reshape(exp_count, capacity, model_width),
        precision=highest,
    )
    scaled_grad = route_sum * norm_gain[None, :]
    projection = jnp.mean(scaled_grad * scaled_input, axis=1, keepdims=True)
    moe_grad = (inverse_rms * (scaled_grad - scaled_input * projection)).astype(jnp.bfloat16)
    moe_heads = lax.all_to_all(moe_grad, "exp", split_axis=1, concat_axis=0, tiled=True)
    moe_float = moe_heads.astype(jnp.float32)
    upstream = grad_float + moe_float
    resid_grad = upstream.astype(jnp.bfloat16)
    upstream_heads = upstream.reshape(token_count, head_count, head_size)
    intra_x, intra_b, local_state = mixer_local(
        upstream_heads,
        inputs_float,
        step_size,
        output_float,
        cumulative,
        decay_matrix,
        intersection,
    )
    total_decay = jnp.exp(cumulative[-1])
    carried = carried_in(
        (total_decay, local_state),
        "ctx",
        chain_combine,
        (jnp.ones_like(total_decay), jnp.zeros_like(local_state)),
    )
    incoming = carried[1]
    tail_decay = jnp.exp(cumulative[-1][None, :] - cumulative)
    grouped_far = incoming.reshape(group_count, head_groups, N, head_size)
    far_x = jnp.einsum("tgn,gjnp->tgjp", input_float, grouped_far, precision=highest).reshape(
        token_count, head_count, head_size
    )
    far_x = far_x * tail_decay[:, :, None]
    mixer_grad = (
        step_size[:, :, None] * (intra_x + far_x) + skip_gain[None, :, None] * upstream_heads
    )
    mixer_grad = mixer_grad.astype(jnp.bfloat16).reshape(token_count, head_count * head_size)
    far_weight = (inputs_float * (step_size * tail_decay)[:, :, None]).reshape(
        token_count, group_count, head_groups, head_size
    )
    far_b = jnp.einsum("gjnp,tgjp->tgn", grouped_far, far_weight, precision=highest)
    state_input_grad = (intra_b + far_b).reshape(token_count, group_count * N)
    return (resid_grad, mixer_grad, state_input_grad)


def solution(mesh):
    in_specs = (
        P(("ctx", "exp"), None),
        P(),
        P(("ctx", "exp"), None),
        P(("ctx", "exp"), None),
        P("exp", "ctx", None),
        P("exp", "ctx", None),
        P("exp", "ctx", None),
        P("ctx", "exp"),
        P("ctx", "exp"),
        P("ctx", "exp"),
        P("ctx", "exp"),
        P("ctx", "exp"),
        P("ctx", "exp"),
        P("exp"),
    )
    out_specs = (P("ctx", "exp"), P("ctx", "exp"), P("ctx", "exp"))
    return jax.shard_map(body, mesh=mesh, in_specs=in_specs, out_specs=out_specs, check_vma=False)
```

profile of v0, /device:TPU:0, one launch (start us, length us, event | category | flops | bytes accessed | tf_op | source)
XLA Modules:
  0.0 321.4 jit_solution(16942792425635660093)
XLA Ops:
  7.2 1.1 fusion.52
  8.3 1.7 fusion.47
  10.8 10.6 %all-gather = s32[8,16,2]{1,2,0:T(2,128)S(1)} all-gather(s32[1,16,2]{1,2,0:T(2,128)} %bitcast.167), channel_id=1, replica_groups=mesh['ctx'=4,'exp'=8] {'exp'}, dimensions={0}, use_global_device_ids=true | all-gather | bytes 1152 | tf_op jit(solution)/shard_map/all_gather | solution.py:132
  22.7 13.9 %all-gather.13.cloned.1.call-done = bf16[128,4096]{1,0:T(8,128)(2,1)} async-done(((bf16[16,4096]{1,0:T(8,128)(2,1)}), bf16[128,4096]{1,0:T(8,128)(2,1)}) %all-gather.13.cloned.1.call-update) | async-done | bytes 1048592 | tf_op jit(solution)/shard_map/all_gather | solution.py:129
  36.6 2.3 convolution_convert_fusion
  39.0 23.0 %all-gather.9.cloned.1.call-done = bf16[128,4096]{1,0:T(8,128)(2,1)} async-done(((bf16[128,512]{1,0:T(8,128)(2,1)}), bf16[128,4096]{1,0:T(8,128)(2,1)}) %all-gather.9.cloned.1.call-update) | async-done | bytes 1048592 | tf_op jit(solution)/shard_map/all_gather | solution.py:121
  62.0 2.3 convolution_convert_fusion.1
  64.6 8.7 %all-gather.1 = bf16[8,16,2]{1,2,0:T(2,128)(2,1)S(1)} all-gather(bf16[1,16,2]{1,2,0:T(2,128)(2,1)S(1)} %bitcast.169), channel_id=1, replica_groups=mesh['ctx'=4,'exp'=8] {'exp'}, dimensions={0}, use_global_device_ids=true | all-gather | bytes 576 | tf_op jit(solution)/shard_map/all_gather | solution.py:130
  75.3 12.5 %all-reduce = bf16[256]{0:T(256)(128)(2,1)S(1)} all-reduce(bf16[256]{0:T(256)(128)(2,1)S(1)} %dynamic-update-slice), channel_id=1, replica_groups=mesh['ctx'=4,'exp'=8] {'ctx'}, use_global_device_ids=true, to_apply=%add | all-reduce | flops 256 | bytes 1024
  87.8 21.7 %all-gather.15.cloned.1.call-done = bf16[256,4096]{1,0:T(8,128)(2,1)} async-done(((bf16[64,4096]{1,0:T(8,128)(2,1)}), bf16[256,4096]{1,0:T(8,128)(2,1)}) %all-gather.15.cloned.1.call-update) | async-done | bytes 2097168 | tf_op jit(solution)/shard_map/all_gather | solution.py:147
  109.5 9.8 %fusion.2 = f32[256,1536]{1,0:T(8,128)} fusion(bf16[256,4096]{1,0:T(8,128)(2,1)} %all-gather.15.cloned.1.call-done, bf16[1,1536,4096]{2,1,0:T(8,128)(2,1)} %param.20), kind=kOutput, calls=%fused_computation.5 | convolution fusion | flops 3221225472 | bytes 16252928 | tf_op jit(solution)/shard_map/dot_general | solution.py:155
  119.3 36.1 %all-gather.11.cloned.1.call-done = bf16[256,4096]{1,0:T(8,128)(2,1)} async-done(((bf16[64,4096]{1,0:T(8,128)(2,1)}), bf16[256,4096]{1,0:T(8,128)(2,1)}) %all-gather.11.cloned.1.call-update) | async-done | bytes 2097168 | tf_op jit(solution)/shard_map/all_gather | solution.py:148
  155.4 9.9 %fusion.17 = f32[256,1536]{1,0:T(8,128)} fusion(bf16[256,4096]{1,0:T(8,128)(2,1)} %all-gather.11.cloned.1.call-done, bf16[1,1536,4096]{2,1,0:T(8,128)(2,1)} %param.22, f32[256]{0:T(256)S(1)} %convert_element_type.157), kind=kOutput, calls=%fused_computation.19 | convolution fusion | flops 3221618688 | bytes 16253952 | tf_op jit(solution)/shard_map/dot_general | solution.py:157
  165.3 16.3 %fusion = f32[256,4096]{1,0:T(8,128)} fusion(bf16[1,1536,4096]{2,1,0:T(8,128)(2,1)} %param.20, f32[256,1536]{1,0:T(8,128)} %fusion.17, bf16[256,4096]{1,0:T(8,128)(2,1)S(1)} %copy-done.10, bf16[1,1536,4096]{2,1,0:T(8,128)(2,1)} %param.21, f32[256,1536]{1,0:T(8,128)} %fusion.2), kind=kOutput, calls=%fused_computation.3 | convolution fusion | flops 6446383104 | bytes 34603008 | tf_op jit(solution)/shard_map/dot_general | solution.py:168
  181.6 11.5 %fusion.13 = bf16[256,4096]{1,0:T(8,128)(2,1)} fusion(f32[256,4096]{1,0:T(8,128)} %fusion, bf16[1,1536,4096]{2,1,0:T(8,128)(2,1)} %param.21, f32[256,1536]{1,0:T(8,128)} %fusion.17, f32[256,1536]{1,0:T(8,128)} %fusion.2), kind=kOutput, calls=%fused_computation.14 | convolution fusion | flops 3225681920 | bytes 22020096 | tf_op jit(solution)/shard_map/dot_general | solution.py:169
  193.2 42.6 %reduce-scatter.2.cloned.1.call-done = bf16[64,4096]{1,0:T(8,128)(2,1)} async-done(((bf16[256,4096]{1,0:T(8,128)(2,1)}), bf16[64,4096]{1,0:T(8,128)(2,1)}) %reduce-scatter.2.cloned.1.call-update) | async-done | bytes 524304 | tf_op jit(solution)/shard_map/reduce_scatter | solution.py:166
  235.8 1.2 reduce-window.15
  238.7 34.7 %all-gather.17.cloned.1.call-done = bf16[512,4096]{1,0:T(8,128)(2,1)} async-done(((bf16[64,4096]{1,0:T(8,128)(2,1)}), bf16[512,4096]{1,0:T(8,128)(2,1)}) %all-gather.17.cloned.1.call-update) | async-done | bytes 4194320 | tf_op jit(solution)/shard_map/all_gather | solution.py:180
  273.4 3.0 fusion.48
  277.3 3.4 %all-to-all-start = ((bf16[16,8,512]{2,0,1:T(8,128)(2,1)}), bf16[16,8,512]{2,0,1:T(8,128)(2,1)S(1)}, u32[]{:S(2)}, u32[]{:S(2)}) async-start(bf16[16,8,512]{2,0,1:T(8,128)(2,1)} %bitcast.136), calls=%async_computation.1 | async-start | bytes 262144 | tf_op jit(solution)/shard_map/all_to_all | solution.py:193
  280.8 10.9 %all-gather.2 = bf16[4,1,8]{2,1,0:T(2,128)(2,1)S(1)} all-gather(bf16[1,1,8]{2,1,0:T(2,128)(2,1)S(1)} %get-tuple-element.139), channel_id=1, replica_groups=mesh['ctx'=4,'exp'=8] {'ctx'}, dimensions={0}, use_global_device_ids=true | all-gather | bytes 80 | tf_op jit(solution)/shard_map/all_gather | solution.py:17
  293.2 14.9 %all_gather.40 = bf16[4,8,128,64]{2,3,1,0:T(8,128)(2,1)S(1)} all-gather(bf16[1,8,128,64]{2,3,1,0:T(8,128)(2,1)S(1)} %bitcast.153), channel_id=1, replica_groups=mesh['ctx'=4,'exp'=8] {'ctx'}, dimensions={0}, use_global_device_ids=true | all-gather | bytes 655360 | tf_op jit(solution)/shard_map/all_gather | solution.py:17
  308.2 1.2 while.14
  312.4 1.2 fusion.38
  (133 shorter events, 12.8 us)
Async XLA Ops:
  7.2 29.4 %all-gather.13.cloned.1.call-start = ((), (), s32[]{:S(2)}) async-start(), calls=%async_computation.4 | async-start | bytes 1179648 | tf_op jit(solution)/shard_map/all_gather | solution.py:129
  10.0 52.0 %all-gather.9.cloned.1.call-start = ((), (), s32[]{:S(2)}) async-start(), calls=%async_computation.2 | async-start | bytes 1179648 | tf_op jit(solution)/shard_map/all_gather | solution.py:121
  10.7 98.8 %all-gather.15.cloned.1.call-start = ((), (), s32[]{:S(2)}) async-start(), calls=%async_computation.5 | async-start | bytes 2621440 | tf_op jit(solution)/shard_map/all_gather | solution.py:147
  22.6 42.0 %copy-start.8 = (bf16[16,2]{0,1:T(2,128)(2,1)S(1)}, bf16[16,2]{0,1:T(2,128)(2,1)}, u32[]{:S(2)}) copy-start(bf16[16,2]{0,1:T(2,128)(2,1)} %param.19) | copy-start | bytes 196
  22.7 51.0 %copy-start.11 = (u32[32]{0:T(128)S(1)}, u32[32]{0:T(128)}, u32[]{:S(2)}) copy-start(u32[32]{0:T(128)} %constant.95) | copy-start | bytes 388
  38.9 116.5 %all-gather.11.cloned.1.call-start = ((), (), s32[]{:S(2)}) async-start(), calls=%async_computation.3 | async-start | bytes 2621440 | tf_op jit(solution)/shard_map/all_gather | solution.py:148
  64.3 171.5 %reduce-scatter.2.cloned.1.call-start = ((), (), s32[]{:S(2)}) async-start(), calls=%async_computation.6 | async-start | bytes 2621440 | tf_op jit(solution)/shard_map/reduce_scatter | solution.py:166
  119.3 46.0 %copy-start.10 = (bf16[256,4096]{1,0:T(8,128)(2,1)S(1)}, bf16[256,4096]{1,0:T(8,128)(2,1)}, u32[]{:S(2)}) copy-start(bf16[256,4096]{1,0:T(8,128)(2,1)} %all-gather.15.cloned.1.call-done) | copy-start | bytes 6291460
  193.2 44.9 %copy-start.7 = (f32[128,8]{0,1:T(8,128)S(1)}, f32[128,8]{0,1:T(8,128)}, u32[]{:S(2)}) copy-start(f32[128,8]{0,1:T(8,128)} %param.28) | copy-start | bytes 12292
  193.2 45.0 %copy-start.6 = (f32[128,8]{0,1:T(8,128)S(1)}, f32[128,8]{0,1:T(8,128)}, u32[]{:S(2)}) copy-start(f32[128,8]{0,1:T(8,128)} %param.27) | copy-start | bytes 12292
  193.2 45.1 %copy-start.5 = (bf16[128,256]{1,0:T(8,128)(2,1)S(1)}, bf16[128,256]{1,0:T(8,128)(2,1)}, u32[]{:S(2)}) copy-start(bf16[128,256]{1,0:T(8,128)(2,1)} %param.26) | copy-start | bytes 196612
  193.2 80.2 %copy-start = (bf16[16,4096]{1,0:T(8,128)(2,1)S(1)}, bf16[16,4096]{1,0:T(8,128)(2,1)}, u32[]{:S(2)}) copy-start(bf16[16,4096]{1,0:T(8,128)(2,1)} %param.16) | copy-start | bytes 393220
  193.2 80.2 %copy-start.4 = (f32[4096]{0:T(1024)S(1)}, f32[4096]{0:T(1024)}, u32[]{:S(2)}) copy-start(f32[4096]{0:T(1024)} %param.17) | copy-start | bytes 49156
  193.2 80.2 %all-gather.17.cloned.1.call-start = ((), (), s32[]{:S(2)}) async-start(), calls=%async_computation.7 | async-start | bytes 4718592 | tf_op jit(solution)/shard_map/all_gather | solution.py:180
  273.4 7.3 %copy-start.2 = (bf16[128,256]{1,0:T(8,128)(2,1)S(1)}, bf16[128,256]{1,0:T(8,128)(2,1)}, u32[]{:S(2)}) copy-start(bf16[128,256]{1,0:T(8,128)(2,1)} %param.25) | copy-start | bytes 196612
  273.4 18.4 %copy-start.3 = (bf16[128,512]{1,0:T(8,128)(2,1)S(1)}, bf16[128,512]{1,0:T(8,128)(2,1)}, u32[]{:S(2)}) copy-start(bf16[128,512]{1,0:T(8,128)(2,1)} %param.24) | copy-start | bytes 393220
  276.4 16.2 %copy-start.9 = (f32[8]{0:T(128)S(1)}, f32[8]{0:T(128)}, u32[]{:S(2)}) copy-start(f32[8]{0:T(128)} %param.29) | copy-start | bytes 100
  276.4 16.3 %copy-start.1 = (bf16[128,512]{1,0:T(8,128)(2,1)S(1)}, bf16[128,512]{1,0:T(8,128)(2,1)}, u32[]{:S(2)}) copy-start(bf16[128,512]{1,0:T(8,128)(2,1)} %param.23) | copy-start | bytes 393220
  277.3 15.5 %all-to-all-start = ((bf16[16,8,512]{2,0,1:T(8,128)(2,1)}), bf16[16,8,512]{2,0,1:T(8,128)(2,1)S(1)}, u32[]{:S(2)}, u32[]{:S(2)}) async-start(bf16[16,8,512]{2,0,1:T(8,128)(2,1)} %bitcast.136), calls=%async_computation.1 | async-start | bytes 262144 | tf_op jit(solution)/shard_map/all_to_all | solution.py:193
Sparse Core Ops, SparseCore 0:
  10.4 26.1 all-gather.12
  38.5 23.4 all-gather.8
  63.5 45.9 all-gather.14
  110.9 44.4 all-gather.10
  193.3 42.4 reduce-scatter.1
  237.6 35.7 all-gather.16
where the time goes:
time: 322 us; the launch traced here: 321 us
  waiting for transfers between devices  173 us (54%)
  matrix products  59 us (18%)
  blocking collectives  57.6 us (18%)
  between operations  15.2 us (5%)
  local copies, waits for them, and re-layouts  6.84 us (2%)
  other arithmetic  6.27 us (2%)
  starting transfers between devices  3.62 us (1%)
    reduce_scatter x1, waiting for transfers between devices, body(): lax.psum_scatter((jnp.dot(gate_grad, gate_rows, preferred_element_type=jn...  42.6 us
    all_gather x1, waiting for transfers between devices, body(): lax.all_gather(slot_grad, 'ctx', axis=0, tiled=True)  36.1 us
    all_gather x1, waiting for transfers between devices, body(): lax.all_gather(half_sum.astype(jnp.bfloat16), 'exp', axis=0, tiled=True)  34.7 us
    all_gather x2, blocking collectives, carried_in(): lax.all_gather(a.astype(kind), axis)  25.8 us
    all_gather x1, waiting for transfers between devices, body(): all_grad = lax.all_gather(grad_output, 'exp', axis=1, tiled=True)  23 us
    all_gather x1, waiting for transfers between devices, body(): lax.all_gather(slot_normed, 'ctx', axis=0, tiled=True)  21.7 us
    dot_general x1, matrix products, body(): jnp.dot(gate_grad, gate_rows, preferred_element_type=jnp.float32)  16.3 us
    all_gather x1, waiting for transfers between devices, body(): lax.all_gather(normed_rows, 'exp', axis=0, tiled=True)  13.9 us
  transfers between devices with their start and end apart: 7, of which 6 were waited for; matrix products, arithmetic and copies ran while one was open for 7% of the time, Pallas kernels for 0%

commit v1 on v0

--- a/solution.py
+++ b/solution.py
@@ -1,12 +1,37 @@
+import functools
 from functools import partial
 import jax
 import jax.numpy as jnp
 from jax import lax
 from jax.sharding import PartitionSpec as P
+from jax.lax import axis_index, axis_size, ppermute
 
 N = 128
 highest = lax.Precision.HIGHEST
 norm_epsilon = 1e-05
+
+
+def bind_ladders(in_array, mesh_dim):
+    opened, odd, vec_out = (axis_size(mesh_dim), axis_index(mesh_dim), in_array.shape[0])
+    bank = [pp * opened if no == 0 else pp for no, pp in enumerate(in_array.shape)]
+    out_arr = lax.dynamic_update_slice_in_dim(
+        jnp.zeros(bank, in_array.dtype), in_array, odd * vec_out, axis=0
+    )
+    r1 = raw_out = in_array
+    for tick in range(1, opened // 2 + 1):
+        r1 = ppermute(r1, mesh_dim, [(no, (no + 1) % opened) for no in range(opened)])
+        out_arr = lax.dynamic_update_slice_in_dim(
+            out_arr, r1, (odd - tick) % opened * vec_out, axis=0
+        )
+        if 2 * tick < opened:
+            raw_out = ppermute(raw_out, mesh_dim, [(no, (no - 1) % opened) for no in range(opened)])
+            out_arr = lax.dynamic_update_slice_in_dim(
+                out_arr, raw_out, (odd + tick) % opened * vec_out, axis=0
+            )
+    return out_arr
+
+
+hold_loads = functools.partial(bind_ladders, mesh_dim="exp")
 
 
 def carried_in(shard, axis, join, neutral):
@@ -177,9 +202,7 @@
     )
     token_tables = all_tables.reshape(expert_count, capacity, row_tokens, 2).sum(axis=3)
     own_tables = lax.dynamic_slice_in_dim(token_tables, exp_index * token_rows, token_rows, 2)
-    parts = lax.all_gather(half_sum.astype(jnp.bfloat16), "exp", axis=0, tiled=True).astype(
-        half_sum.dtype
-    )
+    parts = hold_loads(half_sum.astype(jnp.bfloat16)).astype(half_sum.dtype)
     owner_tables = jnp.repeat(own_tables, 2, axis=0).astype(jnp.float32)
     route_sum = jnp.einsum(
         "xct,xcd->td",

time: 322 us -> 333 us (1.034)
  starting transfers between devices: 3.62 us -> 12.6 us
  waiting for transfers between devices: 173 us -> 178 us
    ppermute x0 -> x7, waiting for transfers between devices: none -> 42.3 us  [the longest x4 42.3 us: bind_ladders(): ppermute(r1, mesh_dim, [(no, (no + 1) % opened) for no in range(opened)])]
    all_gather x1 -> x0, waiting for transfers between devices: 34.7 us -> none  [body(): lax.all_gather(half_sum.astype(jnp.bfloat16), 'exp', axis=0, tiled=True)]
    ppermute x0 -> x7, starting transfers between devices: none -> 7.95 us  [the longest x3 7.94 us: bind_ladders(): ppermute(raw_out, mesh_dim, [(no, (no - 1) % opened) for no in range(open...]
  transfers between devices with their start and end apart: 7 -> 13, of which waited for: 6 -> 9; matrix products, arithmetic and copies ran while one was open for 7% -> 7% of each run, Pallas kernels for 0% -> 0%
where the time goes in v1:
time: 333 us
  waiting for transfers between devices  178 us (53%)
  matrix products  56.8 us (17%)
  blocking collectives  56.3 us (17%)
  between operations  15.1 us (5%)
  starting transfers between devices  12.6 us (4%)
  local copies, waits for them, and re-layouts  7.65 us (2%)
  other arithmetic  6.27 us (2%)
    ppermute x4, waiting for transfers between devices, bind_ladders(): ppermute(r1, mesh_dim, [(no, (no + 1) % opened) for no in range(opened)])  42.3 us
    reduce_scatter x1, waiting for transfers between devices, body(): lax.psum_scatter((jnp.dot(gate_grad, gate_rows, preferred_element_type=jn...  40 us
    all_gather x1, waiting for transfers between devices, body(): lax.all_gather(slot_grad, 'ctx', axis=0, tiled=True)  36.1 us
    all_gather x2, blocking collectives, carried_in(): lax.all_gather(a.astype(kind), axis)  24.6 us
    all_gather x1, waiting for transfers between devices, body(): all_grad = lax.all_gather(grad_output, 'exp', axis=1, tiled=True)  23 us
    all_gather x1, waiting for transfers between devices, body(): lax.all_gather(slot_normed, 'ctx', axis=0, tiled=True)  21.7 us
    dot_general x1, matrix products, body(): jnp.dot(gate_grad, gate_rows, preferred_element_type=jnp.float32)  16.3 us
    all_gather x1, waiting for transfers between devices, body(): lax.all_gather(normed_rows, 'exp', axis=0, tiled=True)  13.9 us
  transfers between devices with their start and end apart: 13, of which 9 were waited for; matrix products, arithmetic and copies ran while one was open for 7% of the time, Pallas kernels for 0%

profile of v1, /device:TPU:0, one launch (start us, length us, event | category | flops | bytes accessed | tf_op | source)
XLA Modules:
  0.0 332.7 jit_solution(12296967862989923678)
XLA Ops:
  10.8 10.6 %all-gather = s32[8,16,2]{1,2,0:T(2,128)S(1)} all-gather(s32[1,16,2]{1,2,0:T(2,128)} %bitcast.167), channel_id=1, replica_groups=mesh['ctx'=4,'exp'=8] {'exp'}, dimensions={0}, use_global_device_ids=true | all-gather | bytes 1152 | tf_op jit(solution)/shard_map/all_gather | solution.py:157
  22.7 13.9 %all-gather.12.cloned.1.call-done = bf16[128,4096]{1,0:T(8,128)(2,1)} async-done(((bf16[16,4096]{1,0:T(8,128)(2,1)}), bf16[128,4096]{1,0:T(8,128)(2,1)}) %all-gather.12.cloned.1.call-update) | async-done | bytes 1048592 | tf_op jit(solution)/shard_map/all_gather | solution.py:154
  36.6 2.3 convolution_convert_fusion
  39.0 23.0 %all-gather.8.cloned.1.call-done = bf16[128,4096]{1,0:T(8,128)(2,1)} async-done(((bf16[128,512]{1,0:T(8,128)(2,1)}), bf16[128,4096]{1,0:T(8,128)(2,1)}) %all-gather.8.cloned.1.call-update) | async-done | bytes 1048592 | tf_op jit(solution)/shard_map/all_gather | solution.py:146
  62.0 2.3 convolution_convert_fusion.1
  64.7 8.7 %all-gather.1 = bf16[8,16,2]{1,2,0:T(2,128)(2,1)S(1)} all-gather(bf16[1,16,2]{1,2,0:T(2,128)(2,1)S(1)} %bitcast.169), channel_id=1, replica_groups=mesh['ctx'=4,'exp'=8] {'exp'}, dimensions={0}, use_global_device_ids=true | all-gather | bytes 576 | tf_op jit(solution)/shard_map/all_gather | solution.py:155
  75.4 12.4 %all-reduce = bf16[256]{0:T(256)(128)(2,1)S(1)} all-reduce(bf16[256]{0:T(256)(128)(2,1)S(1)} %dynamic-update-slice), channel_id=1, replica_groups=mesh['ctx'=4,'exp'=8] {'ctx'}, use_global_device_ids=true, to_apply=%add | all-reduce | flops 256 | bytes 1024
  87.8 21.7 %all-gather.14.cloned.1.call-done = bf16[256,4096]{1,0:T(8,128)(2,1)} async-done(((bf16[64,4096]{1,0:T(8,128)(2,1)}), bf16[256,4096]{1,0:T(8,128)(2,1)}) %all-gather.14.cloned.1.call-update) | async-done | bytes 2097168 | tf_op jit(solution)/shard_map/all_gather | solution.py:172
  109.5 9.8 %fusion.2 = f32[256,1536]{1,0:T(8,128)} fusion(bf16[256,4096]{1,0:T(8,128)(2,1)} %all-gather.14.cloned.1.call-done, bf16[1,1536,4096]{2,1,0:T(8,128)(2,1)} %param.20), kind=kOutput, calls=%fused_computation.5 | convolution fusion | flops 3221225472 | bytes 16252928 | tf_op jit(solution)/shard_map/dot_general | solution.py:180
  119.3 36.1 %all-gather.10.cloned.1.call-done = bf16[256,4096]{1,0:T(8,128)(2,1)} async-done(((bf16[64,4096]{1,0:T(8,128)(2,1)}), bf16[256,4096]{1,0:T(8,128)(2,1)}) %all-gather.10.cloned.1.call-update) | async-done | bytes 2097168 | tf_op jit(solution)/shard_map/all_gather | solution.py:173
  155.4 9.9 %fusion.17 = f32[256,1536]{1,0:T(8,128)} fusion(bf16[256,4096]{1,0:T(8,128)(2,1)} %all-gather.10.cloned.1.call-done, bf16[1,1536,4096]{2,1,0:T(8,128)(2,1)} %param.22, f32[256]{0:T(256)S(1)} %convert_element_type.157), kind=kOutput, calls=%fused_computation.19 | convolution fusion | flops 3221618688 | bytes 16253952 | tf_op jit(solution)/shard_map/dot_general | solution.py:182
  165.3 16.3 %fusion = f32[256,4096]{1,0:T(8,128)} fusion(bf16[1,1536,4096]{2,1,0:T(8,128)(2,1)} %param.20, f32[256,1536]{1,0:T(8,128)} %fusion.17, bf16[256,4096]{1,0:T(8,128)(2,1)S(1)} %copy-done.11, bf16[1,1536,4096]{2,1,0:T(8,128)(2,1)} %param.21, f32[256,1536]{1,0:T(8,128)} %fusion.2), kind=kOutput, calls=%fused_computation.3 | convolution fusion | flops 6446383104 | bytes 34603008 | tf_op jit(solution)/shard_map/dot_general | solution.py:193
  181.7 11.5 %fusion.13 = bf16[256,4096]{1,0:T(8,128)(2,1)} fusion(f32[256,4096]{1,0:T(8,128)} %fusion, bf16[1,1536,4096]{2,1,0:T(8,128)(2,1)} %param.21, f32[256,1536]{1,0:T(8,128)} %fusion.17, f32[256,1536]{1,0:T(8,128)} %fusion.2), kind=kOutput, calls=%fused_computation.14 | convolution fusion | flops 3225681920 | bytes 22020096 | tf_op jit(solution)/shard_map/dot_general | solution.py:194
  195.8 40.0 %reduce-scatter.2.cloned.1.call-done = bf16[64,4096]{1,0:T(8,128)(2,1)} async-done(((bf16[256,4096]{1,0:T(8,128)(2,1)}), bf16[64,4096]{1,0:T(8,128)(2,1)}) %reduce-scatter.2.cloned.1.call-update) | async-done | bytes 524304 | tf_op jit(solution)/shard_map/reduce_scatter | solution.py:191
  235.8 2.6 collective-permute-start.1
  239.4 9.9 %collective-permute-done = bf16[64,4096]{1,0:T(8,128)(2,1)S(1)} collective-permute-done((bf16[64,4096]{1,0:T(8,128)(2,1)}, bf16[64,4096]{1,0:T(8,128)(2,1)S(1)}, u32[]{:S(2)}, u32[]{:S(2)}) %collective-permute-start) | collective-permute-done | bytes 524320 | tf_op jit(solution)/shard_map/ppermute | solution.py:22
  249.4 2.7 collective-permute-start.3
  252.1 11.2 %collective-permute-done.2 = bf16[64,4096]{1,0:T(8,128)(2,1)S(1)} collective-permute-done((bf16[64,4096]{1,0:T(8,128)(2,1)S(1)}, bf16[64,4096]{1,0:T(8,128)(2,1)S(1)}, u32[]{:S(2)}, u32[]{:S(2)}) %collective-permute-start.2) | collective-permute-done | bytes 524320 | tf_op jit(solution)/shard_map/ppermute | solution.py:22
  263.3 2.6 collective-permute-start.5
  266.1 11.8 %collective-permute-done.4 = bf16[64,4096]{1,0:T(8,128)(2,1)S(1)} collective-permute-done((bf16[64,4096]{1,0:T(8,128)(2,1)S(1)}, bf16[64,4096]{1,0:T(8,128)(2,1)S(1)}, u32[]{:S(2)}, u32[]{:S(2)}) %collective-permute-start.4) | collective-permute-done | bytes 524320 | tf_op jit(solution)/shard_map/ppermute | solution.py:22
  278.0 9.4 %collective-permute-done.6 = bf16[64,4096]{1,0:T(8,128)(2,1)S(1)} collective-permute-done((bf16[64,4096]{1,0:T(8,128)(2,1)S(1)}, bf16[64,4096]{1,0:T(8,128)(2,1)S(1)}, u32[]{:S(2)}, u32[]{:S(2)}) %collective-permute-start.6) | collective-permute-done | bytes 524320 | tf_op jit(solution)/shard_map/ppermute | solution.py:22
  289.1 4.4 %all-to-all-start = ((bf16[16,8,512]{2,0,1:T(8,128)(2,1)}), bf16[16,8,512]{2,0,1:T(8,128)(2,1)S(1)}, u32[]{:S(2)}, u32[]{:S(2)}) async-start(bf16[16,8,512]{2,0,1:T(8,128)(2,1)} %bitcast.136), calls=%async_computation.1 | async-start | bytes 262144 | tf_op jit(solution)/shard_map/all_to_all | solution.py:216
  293.7 9.4 %all-gather.2 = bf16[4,1,8]{2,1,0:T(2,128)(2,1)S(1)} all-gather(bf16[1,1,8]{2,1,0:T(2,128)(2,1)S(1)} %get-tuple-element.139), channel_id=1, replica_groups=mesh['ctx'=4,'exp'=8] {'ctx'}, dimensions={0}, use_global_device_ids=true | all-gather | bytes 80 | tf_op jit(solution)/shard_map/all_gather | solution.py:42
  304.6 15.2 %all_gather.36 = bf16[4,8,128,64]{2,3,1,0:T(8,128)(2,1)S(1)} all-gather(bf16[1,8,128,64]{2,3,1,0:T(8,128)(2,1)S(1)} %bitcast.153), channel_id=1, replica_groups=mesh['ctx'=4,'exp'=8] {'ctx'}, dimensions={0}, use_global_device_ids=true | all-gather | bytes 655360 | tf_op jit(solution)/shard_map/all_gather | solution.py:42
  (155 shorter events, 20.7 us)
Async XLA Ops:
  7.2 66.5 %copy-start.12 = (u32[32]{0:T(128)S(1)}, u32[32]{0:T(128)}, u32[]{:S(2)}) copy-start(u32[32]{0:T(128)} %constant.146) | copy-start | bytes 388
  7.2 57.5 %copy-start.9 = (bf16[16,2]{0,1:T(2,128)(2,1)S(1)}, bf16[16,2]{0,1:T(2,128)(2,1)}, u32[]{:S(2)}) copy-start(bf16[16,2]{0,1:T(2,128)(2,1)} %param.19) | copy-start | bytes 196
  7.2 29.4 %all-gather.12.cloned.1.call-start = ((), (), s32[]{:S(2)}) async-start(), calls=%async_computation.4 | async-start | bytes 1179648 | tf_op jit(solution)/shard_map/all_gather | solution.py:154
  10.0 52.0 %all-gather.8.cloned.1.call-start = ((), (), s32[]{:S(2)}) async-start(), calls=%async_computation.2 | async-start | bytes 1179648 | tf_op jit(solution)/shard_map/all_gather | solution.py:146
  10.7 98.8 %all-gather.14.cloned.1.call-start = ((), (), s32[]{:S(2)}) async-start(), calls=%async_computation.5 | async-start | bytes 2621440 | tf_op jit(solution)/shard_map/all_gather | solution.py:172
  39.0 116.5 %all-gather.10.cloned.1.call-start = ((), (), s32[]{:S(2)}) async-start(), calls=%async_computation.3 | async-start | bytes 2621440 | tf_op jit(solution)/shard_map/all_gather | solution.py:173
  64.3 171.5 %reduce-scatter.2.cloned.1.call-start = ((), (), s32[]{:S(2)}) async-start(), calls=%async_computation.6 | async-start | bytes 2621440 | tf_op jit(solution)/shard_map/reduce_scatter | solution.py:191
  119.3 46.0 %copy-start.11 = (bf16[256,4096]{1,0:T(8,128)(2,1)S(1)}, bf16[256,4096]{1,0:T(8,128)(2,1)}, u32[]{:S(2)}) copy-start(bf16[256,4096]{1,0:T(8,128)(2,1)} %all-gather.14.cloned.1.call-done) | copy-start | bytes 6291460
  181.6 13.8 %copy-start.7 = (f32[128,8]{0,1:T(8,128)S(1)}, f32[128,8]{0,1:T(8,128)}, u32[]{:S(2)}) copy-start(f32[128,8]{0,1:T(8,128)} %param.27) | copy-start | bytes 12292
  181.6 57.0 %copy-start.6 = (bf16[128,256]{1,0:T(8,128)(2,1)S(1)}, bf16[128,256]{1,0:T(8,128)(2,1)}, u32[]{:S(2)}) copy-start(bf16[128,256]{1,0:T(8,128)(2,1)} %param.26) | copy-start | bytes 196612
  235.8 13.6 %collective-permute-start = (bf16[64,4096]{1,0:T(8,128)(2,1)}, bf16[64,4096]{1,0:T(8,128)(2,1)S(1)}, u32[]{:S(2)}, u32[]{:S(2)}) collective-permute-start(bf16[64,4096]{1,0:T(8,128)(2,1)} %reduce-scatter.2.cloned.1.call-done), channel_id=1, source_target_pairs={{0,1},{1,2},{2,3},{3,4},{4,5},{5,6},{6,7},{7,0},{8,9},{9,10},{10,1... | collective-permute-start | bytes 1572872 | tf_op jit(solution)/shard_map/ppermute | solution.py:22
  235.8 13.6 %collective-permute-start.1 = (bf16[64,4096]{1,0:T(8,128)(2,1)}, bf16[64,4096]{1,0:T(8,128)(2,1)S(1)}, u32[]{:S(2)}, u32[]{:S(2)}) collective-permute-start(bf16[64,4096]{1,0:T(8,128)(2,1)} %reduce-scatter.2.cloned.1.call-done), channel_id=1, source_target_pairs={{0,7},{1,0},{2,1},{3,2},{4,3},{5,4},{6,5},{7,6},{8,15},{9,8},{10,9... | collective-permute-start | bytes 1572872 | tf_op jit(solution)/shard_map/ppermute | solution.py:27
  239.4 48.1 %copy-start = (bf16[16,4096]{1,0:T(8,128)(2,1)S(1)}, bf16[16,4096]{1,0:T(8,128)(2,1)}, u32[]{:S(2)}) copy-start(bf16[16,4096]{1,0:T(8,128)(2,1)} %param.16) | copy-start | bytes 393220
  239.4 48.1 %copy-start.5 = (f32[4096]{0:T(1024)S(1)}, f32[4096]{0:T(1024)}, u32[]{:S(2)}) copy-start(f32[4096]{0:T(1024)} %param.17) | copy-start | bytes 49156
  249.4 13.9 %collective-permute-start.2 = (bf16[64,4096]{1,0:T(8,128)(2,1)S(1)}, bf16[64,4096]{1,0:T(8,128)(2,1)S(1)}, u32[]{:S(2)}, u32[]{:S(2)}) collective-permute-start(bf16[64,4096]{1,0:T(8,128)(2,1)S(1)} %collective-permute-done), channel_id=1, source_target_pairs={{0,1},{1,2},{2,3},{3,4},{4,5},{5,6},{6,7},{7,0},{8,9},{9,10},{10,1... | collective-permute-start | bytes 1572872 | tf_op jit(solution)/shard_map/ppermute | solution.py:22
  249.4 13.9 %collective-permute-start.3 = (bf16[64,4096]{1,0:T(8,128)(2,1)S(1)}, bf16[64,4096]{1,0:T(8,128)(2,1)S(1)}, u32[]{:S(2)}, u32[]{:S(2)}) collective-permute-start(bf16[64,4096]{1,0:T(8,128)(2,1)S(1)} %collective-permute-done.1), channel_id=1, source_target_pairs={{0,7},{1,0},{2,1},{3,2},{4,3},{5,4},{6,5},{7,6},{8,15},{9,8},{10,9... | collective-permute-start | bytes 1572872 | tf_op jit(solution)/shard_map/ppermute | solution.py:27
  263.3 14.6 %collective-permute-start.4 = (bf16[64,4096]{1,0:T(8,128)(2,1)S(1)}, bf16[64,4096]{1,0:T(8,128)(2,1)S(1)}, u32[]{:S(2)}, u32[]{:S(2)}) collective-permute-start(bf16[64,4096]{1,0:T(8,128)(2,1)S(1)} %collective-permute-done.2), channel_id=1, source_target_pairs={{0,1},{1,2},{2,3},{3,4},{4,5},{5,6},{6,7},{7,0},{8,9},{9,10},{10,1... | collective-permute-start | bytes 1572872 | tf_op jit(solution)/shard_map/ppermute | solution.py:22
  263.3 14.6 %collective-permute-start.5 = (bf16[64,4096]{1,0:T(8,128)(2,1)S(1)}, bf16[64,4096]{1,0:T(8,128)(2,1)S(1)}, u32[]{:S(2)}, u32[]{:S(2)}) collective-permute-start(bf16[64,4096]{1,0:T(8,128)(2,1)S(1)} %collective-permute-done.3), channel_id=1, source_target_pairs={{0,7},{1,0},{2,1},{3,2},{4,3},{5,4},{6,5},{7,6},{8,15},{9,8},{10,9... | collective-permute-start | bytes 1572872 | tf_op jit(solution)/shard_map/ppermute | solution.py:27
  266.1 27.5 %copy-start.3 = (bf16[128,256]{1,0:T(8,128)(2,1)S(1)}, bf16[128,256]{1,0:T(8,128)(2,1)}, u32[]{:S(2)}) copy-start(bf16[128,256]{1,0:T(8,128)(2,1)} %param.25) | copy-start | bytes 196612
  277.9 9.5 %collective-permute-start.6 = (bf16[64,4096]{1,0:T(8,128)(2,1)S(1)}, bf16[64,4096]{1,0:T(8,128)(2,1)S(1)}, u32[]{:S(2)}, u32[]{:S(2)}) collective-permute-start(bf16[64,4096]{1,0:T(8,128)(2,1)S(1)} %collective-permute-done.4), channel_id=1, source_target_pairs={{0,1},{1,2},{2,3},{3,4},{4,5},{5,6},{6,7},{7,0},{8,9},{9,10},{10,1... | collective-permute-start | bytes 1572872 | tf_op jit(solution)/shard_map/ppermute | solution.py:22
  277.9 25.3 %copy-start.4 = (bf16[128,512]{1,0:T(8,128)(2,1)S(1)}, bf16[128,512]{1,0:T(8,128)(2,1)}, u32[]{:S(2)}) copy-start(bf16[128,512]{1,0:T(8,128)(2,1)} %param.24) | copy-start | bytes 393220
  287.4 16.6 %copy-start.10 = (f32[8]{0:T(128)S(1)}, f32[8]{0:T(128)}, u32[]{:S(2)}) copy-start(f32[8]{0:T(128)} %param.29) | copy-start | bytes 100
  287.4 16.7 %copy-start.1 = (bf16[128,512]{1,0:T(8,128)(2,1)S(1)}, bf16[128,512]{1,0:T(8,128)(2,1)}, u32[]{:S(2)}) copy-start(bf16[128,512]{1,0:T(8,128)(2,1)} %param.23) | copy-start | bytes 393220
  289.1 15.1 %all-to-all-start = ((bf16[16,8,512]{2,0,1:T(8,128)(2,1)}), bf16[16,8,512]{2,0,1:T(8,128)(2,1)S(1)}, u32[]{:S(2)}, u32[]{:S(2)}) async-start(bf16[16,8,512]{2,0,1:T(8,128)(2,1)} %bitcast.136), calls=%async_computation.1 | async-start | bytes 262144 | tf_op jit(solution)/shard_map/all_to_all | solution.py:216
  (2 other events, 17.2 us)
Sparse Core Ops, SparseCore 0:
  10.5 26.1 all-gather.11
  38.5 23.4 all-gather.7
  63.6 45.9 all-gather.13
  110.9 44.4 all-gather.9
  193.3 42.4 reduce-scatter.1
